TPU v7x, 256 devices: a whole 4x4x8 slice. The times are simulated.
256 devices in a mesh: row: 8 (over x, core), col: 32 (over y, z).
Axes of the slice: x: 4, y: 4, z: 8, core: 2. Of those that a mesh axis runs over, the one named last changes fastest.
Arguments:
- frames: bfloat16 [3072, 4096], P('row', 'col'), may hold values from -6 to 6
- gain: float32 [4096], replicated, may hold values from 0.3 to 10
- w_value: bfloat16 [4096, 4096], P('row', 'col'), may hold values from -0.09375 to 0.09375
- w_gate: bfloat16 [4096, 4096], P('row', 'col'), may hold values from -0.09375 to 0.09375
- kernel: float32 [31, 4096], P(None, 'col'), may hold values from -1.5 to 1.5
- bias: float32 [4096], P('col'), may hold values from -3 to 3
- w_out: bfloat16 [4096, 4096], P('row', 'col'), may hold values from -0.09375 to 0.09375
- grad_out: bfloat16 [3072, 4096], P('row', 'col'), may hold values from -6 to 6
Outputs:
- encoded: bfloat16 [3072, 4096], P('row', 'col')
- input_grad: bfloat16 [3072, 4096], P('row', 'col')
- grad_value: float32 [4096, 4096], P('row', 'col')
- grad_gate: float32 [4096, 4096], P('row', 'col')
- grad_kernel: float32 [31, 4096], P(None, 'col')
- grad_bias: float32 [4096], P('col')
- grad_out_weight: float32 [4096, 4096], P('row', 'col')
- grad_gain: float32 [4096], P('col')
All inputs are finite; a program needn't handle non-finite values.
Results may differ from a plain program's by a relative error of at most 0.035.
Values may be sent and summed in bfloat16 or wider, within the bound.
No kernel may reach another device: no remote copies, remote signals or barrier semaphores. Data moves between devices by JAX's collectives and lax.ppermute only.
A program may use at most 128 MiB of HBM per device.

v0:
```python
import jax
import jax.numpy as jnp
from jax import lax
from jax.sharding import PartitionSpec as P

K = 31
LEN = 2048
epsilon = 1e-05


def extended(block, sides, width):
    for axis, dim in sides:
        count = lax.axis_size(axis)
        forward = [(i, i + 1) for i in range(count - 1)]
        backward = [(target, source) for source, target in forward]
        low = lax.ppermute(
            lax.slice_in_dim(block, block.shape[dim] - width, None, axis=dim), axis, forward
        )
        high = lax.ppermute(lax.slice_in_dim(block, 0, width, axis=dim), axis, backward)
        block = jnp.concatenate([low, block, high], axis=dim)
    return block


def tap_masks(positions):
    offsets = jnp.arange(K, dtype=jnp.int32) - K // 2
    placed = (positions % LEN)[None, :] + offsets[:, None]
    return ((placed >= 0) & (placed < LEN)).astype(jnp.float32)


def contract_rows(left, right):
    return lax.dot_general(
        left, right, (((0,), (0,)), ((), ())), preferred_element_type=jnp.float32
    )


def contract_cols(left, right):
    return lax.dot_general(
        left, right, (((1,), (1,)), ((), ())), preferred_element_type=jnp.float32
    )


def shards(frames, gain, w_value, w_gate, kernel, bias, w_out, grad_out):
    row_count = frames.shape[0]
    col_count = frames.shape[1]
    chan_count = w_value.shape[1]
    width = col_count * lax.axis_size("col")
    half_width = K // 2
    row_start = lax.axis_index("row") * row_count
    col_start = lax.axis_index("col") * col_count
    local_gain = lax.dynamic_slice_in_dim(gain, col_start, col_count, 0)
    wide = frames.astype(jnp.float32)
    sum_row, square_sum = lax.psum((jnp.sum(wide, axis=1), jnp.sum(wide * wide, axis=1)), "col")
    mean_row = sum_row / width
    inv_std = lax.rsqrt(square_sum / width - mean_row * mean_row + epsilon)
    centred = (wide - mean_row[:, None]) * inv_std[:, None]
    normed = lax.all_gather(
        (centred * local_gain[None, :]).astype(jnp.bfloat16), "col", axis=1, tiled=True
    )
    value_full, gate_full = (
        lax.all_gather(w_value, "row", axis=0, tiled=True),
        lax.all_gather(w_gate, "row", axis=0, tiled=True),
    )
    value_pre = jnp.dot(normed, value_full, preferred_element_type=jnp.float32)
    gate_pre = jnp.dot(normed, gate_full, preferred_element_type=jnp.float32)
    gate_sig = jax.nn.sigmoid(gate_pre)
    gated = (value_pre * gate_sig).astype(jnp.bfloat16)
    padded_glu = extended(gated, (("row", 0),), half_width).astype(jnp.float32)
    local_masks = tap_masks(row_start + jnp.arange(row_count, dtype=jnp.int32))
    conv_pre = jnp.zeros((row_count, chan_count), jnp.float32) + bias[None, :]
    for tap_index in range(K):
        conv_pre = (
            conv_pre
            + kernel[tap_index][None, :]
            * local_masks[tap_index][:, None]
            * padded_glu[tap_index : tap_index + row_count]
        )
    conv_sig = jax.nn.sigmoid(conv_pre)
    activated = (conv_pre * conv_sig).astype(jnp.bfloat16)
    act_full = lax.all_gather(activated, "col", axis=1, tiled=True)
    out_full = lax.all_gather(w_out, "row", axis=0, tiled=True)
    encoded = (
        frames.astype(jnp.float32) + jnp.dot(act_full, out_full, preferred_element_type=jnp.float32)
    ).astype(jnp.bfloat16)
    act_terms = contract_cols(grad_out, out_full)
    act_grad = lax.psum_scatter(
        act_terms.astype(jnp.bfloat16), "col", scatter_dimension=1, tiled=True
    ).astype(jnp.float32)
    grad_out_weight = lax.psum_scatter(
        contract_rows(act_full, grad_out).astype(jnp.bfloat16),
        "row",
        scatter_dimension=0,
        tiled=True,
    ).astype(jnp.float32)
    conv_grad = (act_grad * conv_sig * (1.0 + conv_pre * (1.0 - conv_sig))).astype(jnp.bfloat16)
    conv_wide = conv_grad.astype(jnp.float32)
    padded_grad = extended(conv_grad, (("row", 0),), half_width).astype(jnp.float32)
    outer_masks = tap_masks(
        row_start - half_width + jnp.arange(row_count + 2 * half_width, dtype=jnp.int32)
    )
    glu_grad = jnp.zeros((row_count, chan_count), jnp.float32)
    kernel_rows = []
    for tap_index in range(K):
        begin = 2 * half_width - tap_index
        glu_grad = (
            glu_grad
            + kernel[tap_index][None, :]
            * outer_masks[tap_index, begin : begin + row_count][:, None]
            * padded_grad[begin : begin + row_count]
        )
        kernel_rows.append(
            jnp.sum(
                local_masks[tap_index][:, None]
                * conv_wide
                * padded_glu[tap_index : tap_index + row_count],
                axis=0,
            )
        )
    kernel_term = jnp.stack(kernel_rows)
    bias_term = jnp.sum(conv_wide, axis=0)
    grad_kernel, grad_bias = lax.psum((kernel_term, bias_term), "row")
    value_grad = (glu_grad * gate_sig).astype(jnp.bfloat16)
    gate_grad = (glu_grad * value_pre * gate_sig * (1.0 - gate_sig)).astype(jnp.bfloat16)
    both_grads = jnp.concatenate([value_grad, gate_grad], axis=1)
    in_weight = lax.psum_scatter(
        contract_rows(normed, both_grads).astype(jnp.bfloat16),
        "row",
        scatter_dimension=0,
        tiled=True,
    ).astype(jnp.float32)
    grad_value = in_weight[:, :chan_count]
    grad_gate = in_weight[:, chan_count:]
    norm_terms = contract_cols(value_grad, value_full) + contract_cols(gate_grad, gate_full)
    normed_grad = lax.psum_scatter(
        norm_terms.astype(jnp.bfloat16), "col", scatter_dimension=1, tiled=True
    ).astype(jnp.float32)
    hat_grad = normed_grad * local_gain[None, :]
    first_sum, second_sum = lax.psum(
        (jnp.sum(hat_grad, axis=1), jnp.sum(hat_grad * centred, axis=1)), "col"
    )
    input_grad = (
        grad_out.astype(jnp.float32)
        + inv_std[:, None]
        * (hat_grad - first_sum[:, None] / width - centred * (second_sum / width)[:, None])
    ).astype(jnp.bfloat16)
    gain_term = jnp.sum(normed_grad * centred, axis=0)
    grad_gain = lax.psum(gain_term, "row")
    return (
        encoded,
        input_grad,
        grad_value,
        grad_gate,
        grad_kernel,
        grad_bias,
        grad_out_weight,
        grad_gain,
    )


def solution(mesh):
    placed = (
        P("row", "col"),
        P(),
        P("row", "col"),
        P("row", "col"),
        P(None, "col"),
        P("col"),
        P("row", "col"),
        P("row", "col"),
    )
    return jax.shard_map(
        shards,
        mesh=mesh,
        in_specs=placed,
        out_specs=(
            P("row", "col"),
            P("row", "col"),
            P("row", "col"),
            P("row", "col"),
            P(None, "col"),
            P("col"),
            P("row", "col"),
            P("col"),
        ),
        check_vma=False,
    )
```

profile of v0, /device:TPU:0, one launch (start us, length us, event | category | flops | bytes accessed | tf_op | source)
XLA Modules:
  0.0 864.5 jit_solution(822775014375690964)
XLA Ops:
  7.2 0.0 all-gather.14.cloned.1.call-start
  7.2 0.7 all-gather.14.cloned.1.call-update
  7.9 0.0 all-gather.10.cloned.1.call-start
  7.9 0.7 all-gather.10.cloned.1.call-update
  8.7 0.0 all-gather.6.cloned.1.call-start
  8.7 0.8 dynamic_slice.3
  9.5 1.1 convert_reduce_fusion.1
  10.5 76.2 %all-reduce.1 = (f32[384]{0:T(512)S(1)}, f32[384]{0:T(512)S(1)}) all-reduce(f32[384]{0:T(512)S(1)} %get-tuple-element.44, f32[384]{0:T(512)S(1)} %get-tuple-element.43), channel_id=1, replica_groups=mesh['row'=8,'col'=32] {'col'}, use_global_device_ids=true, to_apply=%region_3.0 | all-reduce | flops 768 | bytes 6144 | tf_op jit(solution)/shard_map/psum | solution.py:52
  86.8 0.6 copy-done.9
  87.3 1.7 fusion.16
  89.1 0.0 all-gather.8.cloned.1.call-start
  89.1 0.5 all-gather.8.cloned.1.call-update
  89.6 0.0 reduce-scatter.13.cloned.1.call-start
  89.7 2.3 convolution_convert_fusion
  92.0 2.8 copy.16
  94.8 0.0 all-gather.12.cloned.1.call-start
  94.9 0.1 fusion.116
  95.0 0.4 copy-done.69
  95.4 0.1 slice_reduce_fusion.61
  95.6 0.6 slice_bitcast_fusion.29
  96.2 0.7 slice_bitcast_fusion.30
  96.9 64.5 %all-gather.6.cloned.1.call-done = bf16[384,4096]{1,0:T(8,128)(2,1)} async-done(((bf16[384,128]{1,0:T(8,128)(2,1)}), bf16[384,4096]{1,0:T(8,128)(2,1)}) %all-gather.6.cloned.1.call-update) | async-done | bytes 3145744 | tf_op jit(solution)/shard_map/all_gather | solution.py:56
  161.4 3.3 fusion.2
  164.8 24.6 %all-gather.8.cloned.1.call-done = bf16[4096,128]{1,0:T(8,128)(2,1)} async-done(((bf16[512,128]{1,0:T(8,128)(2,1)}), bf16[4096,128]{1,0:T(8,128)(2,1)}) %all-gather.8.cloned.1.call-update) | async-done | bytes 1048592 | tf_op jit(solution)/shard_map/all_gather | solution.py:60
  189.4 2.9 multiply_convert_fusion.4
  192.3 2.2 collective-permute-start
  194.4 1.3 collective-permute-start.1
  195.7 0.1 slice_reduce_fusion.60
  195.9 1.6 collective-permute-done.1
  197.5 215.0 %reduce-scatter.13.cloned.1.call-done = bf16[128,384]{1,0:T(8,128)(2,1)} async-done(((bf16[4096,384]{1,0:T(8,128)(2,1)}), bf16[128,384]{1,0:T(8,128)(2,1)}) %reduce-scatter.13.cloned.1.call-update) | async-done | bytes 98320
  412.5 1.0 copy.17
  414.0 4.1 fusion.75
  418.1 0.7 multiply_convert_fusion.3
  418.9 0.0 reduce-scatter.9.cloned.1.call-start
  418.9 0.1 fusion.114
  419.0 0.2 slice_reduce_fusion.30
  419.2 1.3 collective-permute-start.2
  420.5 1.3 collective-permute-start.3
  421.8 0.1 slice_reduce_fusion.29
  421.9 3.3 collective-permute-done.3
  425.6 3.1 multiply_convert_fusion
  428.7 2.6 convolution_convert_fusion.1
  431.4 0.0 reduce-scatter.15.cloned.1.call-start
  431.4 1.0 fusion.124
  432.4 0.2 copy-done.5
  432.7 1.0 add_convert_fusion
  433.6 2.9 copy.18
  436.6 0.2 reduce-scatter.11.cloned.1.call-start
  436.8 58.9 %all-gather.12.cloned.1.call-done = bf16[384,4096]{1,0:T(8,128)(2,1)} async-done(((bf16[384,128]{1,0:T(8,128)(2,1)}), bf16[384,4096]{1,0:T(8,128)(2,1)}) %all-gather.12.cloned.1.call-update) | async-done | bytes 3145744 | tf_op jit(solution)/shard_map/all_gather | solution.py:79
  495.7 3.9 convolution_convert_fusion.2
  499.7 1.7 fusion.73
  501.4 1.9 fusion.77
  503.3 1.9 fusion.79
  505.1 3.0 stack.127
  508.1 26.7 %reduce-scatter.9.cloned.1.call-done = bf16[512,256]{1,0:T(8,128)(2,1)} async-done(((bf16[4096,256]{1,0:T(8,128)(2,1)}), bf16[512,256]{1,0:T(8,128)(2,1)}) %reduce-scatter.9.cloned.1.call-update) | async-done | bytes 262160 | tf_op jit(solution)/shard_map/reduce_scatter | solution.py:124
  534.8 1.8 fusion.121
  536.6 2.9 fusion.3
  539.5 218.2 %reduce-scatter.15.cloned.1.call-done = bf16[128,384]{1,0:T(8,128)(2,1)} async-done(((bf16[4096,384]{1,0:T(8,128)(2,1)}), bf16[128,384]{1,0:T(8,128)(2,1)}) %reduce-scatter.15.cloned.1.call-update) | async-done | bytes 98320
  757.7 1.0 copy.19
  758.7 0.3 fusion.12
  759.0 72.2 %all-reduce = (f32[384]{0:T(512)S(1)}, f32[384]{0:T(512)S(1)}) all-reduce(f32[384]{0:T(512)S(1)} %get-tuple-element.40, f32[384]{0:T(512)S(1)} %get-tuple-element.41), channel_id=1, replica_groups=mesh['row'=8,'col'=32] {'col'}, use_global_device_ids=true, to_apply=%region_9.10 | all-reduce | flops 768 | bytes 6144 | tf_op jit(solution)/shard_map/psum | solution.py:137
  831.2 24.2 %all-reduce.2 = (f32[31,128]{1,0:T(8,128)}, f32[128]{0:T(128)}, f32[128]{0:T(128)}) all-reduce(f32[31,128]{1,0:T(8,128)S(1)} %stack.127, f32[128]{0:T(128)S(1)} %copy-done.71, f32[128]{0:T(128)S(1)} %get-tuple-element.39), channel_id=1, replica_groups=mesh['row'=8,'col'=32] {'row'}, use_global_device_ids=true, to_apply=%region_42.43 | all-reduce | flops 4224 | bytes 33792 | tf_op jit(solution)/shard_map/psum | solution.py:120
  855.4 0.9 fusion.10
  856.3 1.6 convert_element_type.92
  (162 shorter events, 0.6 us)
Async XLA Ops:
  7.2 82.6 %all-gather.14.cloned.1.call-start = ((), (), s32[]{:S(2)}) async-start(), calls=%async_computation.8 | async-start | bytes 1179648 | tf_op jit(solution)/shard_map/all_gather | solution.py:80
  7.9 89.0 %all-gather.10.cloned.1.call-start = ((), (), s32[]{:S(2)}) async-start(), calls=%async_computation.6 | async-start | bytes 1179648 | tf_op jit(solution)/shard_map/all_gather | solution.py:61
  8.7 152.8 %all-gather.6.cloned.1.call-start = ((), (), s32[]{:S(2)}) async-start(), calls=%async_computation.4 | async-start | bytes 3244032 | tf_op jit(solution)/shard_map/all_gather | solution.py:56
  9.5 80.2 %copy-start.36 = (f32[128]{0:T(128)}, f32[128]{0:T(128)S(1)}, u32[]{:S(2)}) copy-start(f32[128]{0:T(128)S(1)} %dynamic_slice.3) | copy-start | bytes 1540
  89.1 100.3 %all-gather.8.cloned.1.call-start = ((), (), s32[]{:S(2)}) async-start(), calls=%async_computation.5 | async-start | bytes 1179648 | tf_op jit(solution)/shard_map/all_gather | solution.py:60
  89.6 322.9 %reduce-scatter.13.cloned.1.call-start = ((), (), s32[]{:S(2)}) async-start(), calls=%async_computation.11 | async-start | bytes 3244032
  94.8 400.9 %all-gather.12.cloned.1.call-start = ((), (), s32[]{:S(2)}) async-start(), calls=%async_computation.7 | async-start | bytes 3244032 | tf_op jit(solution)/shard_map/all_gather | solution.py:79
  95.5 318.0 %copy-start.13 = (f32[384]{0:T(512)}, f32[384]{0:T(512)S(1)}, u32[]{:S(2)}) copy-start(f32[384]{0:T(512)S(1)} %get-tuple-element.77) | copy-start | bytes 4612
  95.5 318.0 %copy-start.14 = (f32[384]{0:T(512)}, f32[384]{0:T(512)S(1)}, u32[]{:S(2)}) copy-start(f32[384]{0:T(512)S(1)} %get-tuple-element.78) | copy-start | bytes 4612
  95.5 318.0 %copy-start.15 = (f32[384]{0:T(512)}, f32[384]{0:T(512)S(1)}, u32[]{:S(2)}) copy-start(f32[384]{0:T(512)S(1)} %get-tuple-element.91) | copy-start | bytes 4612
  95.5 318.0 %copy-start.16 = (f32[384]{0:T(512)}, f32[384]{0:T(512)S(1)}, u32[]{:S(2)}) copy-start(f32[384]{0:T(512)S(1)} %get-tuple-element.92) | copy-start | bytes 4612
  95.5 318.0 %copy-start.17 = (f32[384]{0:T(512)}, f32[384]{0:T(512)S(1)}, u32[]{:S(2)}) copy-start(f32[384]{0:T(512)S(1)} %get-tuple-element.93) | copy-start | bytes 4612
  95.5 318.0 %copy-start.18 = (f32[384]{0:T(512)}, f32[384]{0:T(512)S(1)}, u32[]{:S(2)}) copy-start(f32[384]{0:T(512)S(1)} %get-tuple-element.94) | copy-start | bytes 4612
  95.5 318.0 %copy-start.19 = (f32[384]{0:T(512)}, f32[384]{0:T(512)S(1)}, u32[]{:S(2)}) copy-start(f32[384]{0:T(512)S(1)} %get-tuple-element.76) | copy-start | bytes 4612
  95.6 318.0 %copy-start.20 = (f32[384]{0:T(512)}, f32[384]{0:T(512)S(1)}, u32[]{:S(2)}) copy-start(f32[384]{0:T(512)S(1)} %get-tuple-element.80) | copy-start | bytes 4612
  95.6 318.0 %copy-start.21 = (f32[384]{0:T(512)}, f32[384]{0:T(512)S(1)}, u32[]{:S(2)}) copy-start(f32[384]{0:T(512)S(1)} %get-tuple-element.81) | copy-start | bytes 4612
  95.6 318.0 %copy-start.22 = (f32[384]{0:T(512)}, f32[384]{0:T(512)S(1)}, u32[]{:S(2)}) copy-start(f32[384]{0:T(512)S(1)} %get-tuple-element.82) | copy-start | bytes 4612
  96.2 317.4 %copy-start.38 = (f32[128]{0:T(128)}, f32[128]{0:T(128)S(1)}, u32[]{:S(2)}) copy-start(f32[128]{0:T(128)S(1)} %get-tuple-element.143) | copy-start | bytes 1540
  96.2 317.4 %copy-start.39 = (f32[128]{0:T(128)}, f32[128]{0:T(128)S(1)}, u32[]{:S(2)}) copy-start(f32[128]{0:T(128)S(1)} %get-tuple-element.144) | copy-start | bytes 1540
  96.2 317.4 %copy-start.40 = (f32[128]{0:T(128)}, f32[128]{0:T(128)S(1)}, u32[]{:S(2)}) copy-start(f32[128]{0:T(128)S(1)} %get-tuple-element.145) | copy-start | bytes 1540
  96.2 317.4 %copy-start.41 = (f32[128]{0:T(128)}, f32[128]{0:T(128)S(1)}, u32[]{:S(2)}) copy-start(f32[128]{0:T(128)S(1)} %get-tuple-element.146) | copy-start | bytes 1540
  96.2 317.4 %copy-start.42 = (f32[128]{0:T(128)}, f32[128]{0:T(128)S(1)}, u32[]{:S(2)}) copy-start(f32[128]{0:T(128)S(1)} %get-tuple-element.147) | copy-start | bytes 1540
  161.4 27.9 %copy-start.2 = (bf16[384,4096]{1,0:T(8,128)(2,1)S(1)}, bf16[384,4096]{1,0:T(8,128)(2,1)}, u32[]{:S(2)}) copy-start(bf16[384,4096]{1,0:T(8,128)(2,1)} %all-gather.6.cloned.1.call-done) | copy-start | bytes 9437188
  192.3 3.7 collective-permute-start
  194.4 3.1 collective-permute-start.1
  195.8 222.2 %copy-start.23 = (f32[384]{0:T(512)}, f32[384]{0:T(512)S(1)}, u32[]{:S(2)}) copy-start(f32[384]{0:T(512)S(1)} %get-tuple-element.95) | copy-start | bytes 4612
  195.8 222.2 %copy-start.24 = (f32[384]{0:T(512)}, f32[384]{0:T(512)S(1)}, u32[]{:S(2)}) copy-start(f32[384]{0:T(512)S(1)} %get-tuple-element.100) | copy-start | bytes 4612
  195.8 222.2 %copy-start.25 = (f32[384]{0:T(512)}, f32[384]{0:T(512)S(1)}, u32[]{:S(2)}) copy-start(f32[384]{0:T(512)S(1)} %get-tuple-element.101) | copy-start | bytes 4612
  195.8 222.2 %copy-start.26 = (f32[384]{0:T(512)}, f32[384]{0:T(512)S(1)}, u32[]{:S(2)}) copy-start(f32[384]{0:T(512)S(1)} %get-tuple-element.102) | copy-start | bytes 4612
  195.8 222.2 %copy-start.27 = (f32[384]{0:T(512)}, f32[384]{0:T(512)S(1)}, u32[]{:S(2)}) copy-start(f32[384]{0:T(512)S(1)} %get-tuple-element.103) | copy-start | bytes 4612
  195.8 222.2 %copy-start.28 = (f32[384]{0:T(512)}, f32[384]{0:T(512)S(1)}, u32[]{:S(2)}) copy-start(f32[384]{0:T(512)S(1)} %get-tuple-element.104) | copy-start | bytes 4612
  195.8 222.2 %copy-start.29 = (f32[384]{0:T(512)}, f32[384]{0:T(512)S(1)}, u32[]{:S(2)}) copy-start(f32[384]{0:T(512)S(1)} %get-tuple-element.105) | copy-start | bytes 4612
  195.9 222.2 %copy-start.30 = (f32[384]{0:T(512)}, f32[384]{0:T(512)S(1)}, u32[]{:S(2)}) copy-start(f32[384]{0:T(512)S(1)} %get-tuple-element.106) | copy-start | bytes 4612
  195.9 222.2 %copy-start.31 = (f32[384]{0:T(512)}, f32[384]{0:T(512)S(1)}, u32[]{:S(2)}) copy-start(f32[384]{0:T(512)S(1)} %get-tuple-element.96) | copy-start | bytes 4612
  195.9 222.2 %copy-start.32 = (f32[384]{0:T(512)}, f32[384]{0:T(512)S(1)}, u32[]{:S(2)}) copy-start(f32[384]{0:T(512)S(1)} %get-tuple-element.97) | copy-start | bytes 4612
  195.9 222.2 %copy-start.33 = (f32[384]{0:T(512)}, f32[384]{0:T(512)S(1)}, u32[]{:S(2)}) copy-start(f32[384]{0:T(512)S(1)} %get-tuple-element.98) | copy-start | bytes 4612
  195.9 222.2 %copy-start.34 = (f32[384]{0:T(512)}, f32[384]{0:T(512)S(1)}, u32[]{:S(2)}) copy-start(f32[384]{0:T(512)S(1)} %get-tuple-element.99) | copy-start | bytes 4612
  413.7 11.6 %copy-start.8 = (f32[384,128]{1,0:T(8,128)S(1)}, f32[384,128]{1,0:T(8,128)}, u32[]{:S(2)}) copy-start(f32[384,128]{1,0:T(8,128)} %get-tuple-element.158) | copy-start | bytes 589828
  413.7 11.6 %copy-start.43 = (f32[128]{0:T(128)S(1)}, f32[128]{0:T(128)}, u32[]{:S(2)}) copy-start(f32[128]{0:T(128)} %get-tuple-element.148) | copy-start | bytes 1540
  413.7 11.6 %copy-start.44 = (f32[128]{0:T(128)S(1)}, f32[128]{0:T(128)}, u32[]{:S(2)}) copy-start(f32[128]{0:T(128)} %get-tuple-element.149) | copy-start | bytes 1540
  413.7 11.6 %copy-start.45 = (f32[128]{0:T(128)S(1)}, f32[128]{0:T(128)}, u32[]{:S(2)}) copy-start(f32[128]{0:T(128)} %get-tuple-element.150) | copy-start | bytes 1540
  413.7 11.6 %copy-start.46 = (f32[128]{0:T(128)S(1)}, f32[128]{0:T(128)}, u32[]{:S(2)}) copy-start(f32[128]{0:T(128)} %get-tuple-element.151) | copy-start | bytes 1540
  413.7 11.6 %copy-start.47 = (f32[128]{0:T(128)S(1)}, f32[128]{0:T(128)}, u32[]{:S(2)}) copy-start(f32[128]{0:T(128)} %get-tuple-element.152) | copy-start | bytes 1540
  413.7 11.6 %copy-start.48 = (f32[128]{0:T(128)S(1)}, f32[128]{0:T(128)}, u32[]{:S(2)}) copy-start(f32[128]{0:T(128)} %get-tuple-element.153) | copy-start | bytes 1540
  413.8 11.6 %copy-start.49 = (f32[128]{0:T(128)S(1)}, f32[128]{0:T(128)}, u32[]{:S(2)}) copy-start(f32[128]{0:T(128)} %get-tuple-element.154) | copy-start | bytes 1540
  413.8 11.6 %copy-start.50 = (f32[128]{0:T(128)S(1)}, f32[128]{0:T(128)}, u32[]{:S(2)}) copy-start(f32[128]{0:T(128)} %get-tuple-element.124) | copy-start | bytes 1540
  413.8 11.6 %copy-start.51 = (f32[128]{0:T(128)S(1)}, f32[128]{0:T(128)}, u32[]{:S(2)}) copy-start(f32[128]{0:T(128)} %get-tuple-element.125) | copy-start | bytes 1540
  413.8 11.6 %copy-start.52 = (f32[128]{0:T(128)S(1)}, f32[128]{0:T(128)}, u32[]{:S(2)}) copy-start(f32[128]{0:T(128)} %get-tuple-element.126) | copy-start | bytes 1540
  413.8 11.6 %copy-start.53 = (f32[128]{0:T(128)S(1)}, f32[128]{0:T(128)}, u32[]{:S(2)}) copy-start(f32[128]{0:T(128)} %get-tuple-element.127) | copy-start | bytes 1540
  413.8 11.6 %copy-start.54 = (f32[128]{0:T(128)S(1)}, f32[128]{0:T(128)}, u32[]{:S(2)}) copy-start(f32[128]{0:T(128)} %get-tuple-element.128) | copy-start | bytes 1540
  413.8 11.6 %copy-start.55 = (f32[128]{0:T(128)S(1)}, f32[128]{0:T(128)}, u32[]{:S(2)}) copy-start(f32[128]{0:T(128)} %get-tuple-element.129) | copy-start | bytes 1540
  418.9 116.0 %reduce-scatter.9.cloned.1.call-start = ((), (), s32[]{:S(2)}) async-start(), calls=%async_computation.9 | async-start | bytes 2359296 | tf_op jit(solution)/shard_map/reduce_scatter | solution.py:124
  419.2 2.7 collective-permute-start.2
  420.5 4.8 collective-permute-start.3
  431.4 326.3 %reduce-scatter.15.cloned.1.call-start = ((), (), s32[]{:S(2)}) async-start(), calls=%async_computation.12 | async-start | bytes 3244032
  436.5 59.2 %copy-start.6 = (bf16[384,128]{1,0:T(8,128)(2,1)S(1)}, bf16[384,128]{1,0:T(8,128)(2,1)}, u32[]{:S(2)}) copy-start(bf16[384,128]{1,0:T(8,128)(2,1)} %param.15) | copy-start | bytes 294916
  436.6 419.8 %reduce-scatter.11.cloned.1.call-start = ((), (), s32[]{:S(2)}) async-start(), calls=%async_computation.10 | async-start | bytes 1179648 | tf_op jit(solution)/shard_map/reduce_scatter | solution.py:88
  499.6 37.0 %copy-start = (bf16[384,4096]{1,0:T(8,128)(2,1)S(1)}, bf16[384,4096]{1,0:T(8,128)(2,1)}, u32[]{:S(2)}) copy-start(bf16[384,4096]{1,0:T(8,128)(2,1)} %all-gather.12.cloned.1.call-done) | copy-start | bytes 9437188
  499.7 37.0 %copy-start.4 = (bf16[384,128]{1,0:T(8,128)(2,1)S(1)}, bf16[384,128]{1,0:T(8,128)(2,1)}, u32[]{:S(2)}) copy-start(bf16[384,128]{1,0:T(8,128)(2,1)} %param.8) | copy-start | bytes 294916
  505.1 253.6 %copy-start.10 = (f32[384]{0:T(512)S(1)}, f32[384]{0:T(512)}, u32[]{:S(2)}) copy-start(f32[384]{0:T(512)} %copy-done.9) | copy-start | bytes 4612
  505.1 253.6 %copy-start.12 = (f32[384]{0:T(512)S(1)}, f32[384]{0:T(512)}, u32[]{:S(2)}) copy-start(f32[384]{0:T(512)} %copy-done.11) | copy-start | bytes 4612
  505.1 253.6 %copy-start.37 = (f32[128]{0:T(128)S(1)}, f32[128]{0:T(128)}, u32[]{:S(2)}) copy-start(f32[128]{0:T(128)} %copy-done.36) | copy-start | bytes 1540
  505.1 326.1 %copy-start.71 = (f32[128]{0:T(128)S(1)}, f32[128]{0:T(128)}, u32[]{:S(2)}) copy-start(f32[128]{0:T(128)} %get-tuple-element.42) | copy-start | bytes 1540
  505.1 350.3 %copy-start.7 = (bf16[384,128]{1,0:T(8,128)(2,1)S(1)}, bf16[384,128]{1,0:T(8,128)(2,1)}, u32[]{:S(2)}) copy-start(bf16[384,128]{1,0:T(8,128)(2,1)} %param.15) | copy-start | bytes 294916
  (21 other events, 165.7 us)
Sparse Core Ops, SparseCore 0:
  9.9 27.1 all-gather.13
  38.9 25.7 all-gather.9
  89.2 72.2 all-gather.5
  163.2 26.1 all-gather.7
  193.1 219.3 reduce-scatter.12
  419.0 76.6 all-gather.11
  498.4 36.3 reduce-scatter.8
  539.2 218.4 reduce-scatter.14
  760.2 32.8 reduce-scatter.10
where the time goes:
time: 865 us; the launch traced here: 864 us
  waiting for transfers between devices  615 us (71%)
  blocking collectives  173 us (20%)
  matrix products  19.8 us (2%)
  other arithmetic  19.2 us (2%)
  local copies, waits for them, and re-layouts  16.5 us (2%)
  between operations  15 us (2%)
    unnamed x11, waiting for transfers between devices  435 us
    psum x1, blocking collectives, shards(): lax.psum((jnp.sum(wide, axis=1), jnp.sum(wide * wide, axis=1)), 'col')  76.2 us
    psum x1, blocking collectives, shards(): lax.psum((jnp.sum(hat_grad, axis=1), jnp.sum(hat_grad * centred, axis=1))...  72.2 us
    all_gather x1, waiting for transfers between devices, shards(): lax.all_gather((centred * local_gain[None, :]).astype(jnp.bfloat16), 'col...  64.5 us
    all_gather x1, waiting for transfers between devices, shards(): act_full = lax.all_gather(activated, 'col', axis=1, tiled=True)  58.9 us
    reduce_scatter x1, waiting for transfers between devices, shards(): lax.psum_scatter(contract_rows(normed, both_grads).astype(jnp.bfloat16),...  26.7 us
    all_gather x1, waiting for transfers between devices, shards(): lax.all_gather(w_value, 'row', axis=0, tiled=True)  24.6 us
    psum x1, blocking collectives, shards(): grad_kernel, grad_bias = lax.psum((kernel_term, bias_term), 'row')  24.2 us
  transfers between devices with their start and end apart: 13, of which 8 were waited for; matrix products, arithmetic and copies ran while one was open for 5% of the time, Pallas kernels for 0%

commit v1 on v0

--- a/solution.py
+++ b/solution.py
@@ -6,6 +6,13 @@
 K = 31
 LEN = 2048
 epsilon = 1e-05
+
+
+def view_node(w_in):
+    n_slots = lax.axis_size("row")
+    heap = tuple((n_slots if dev_i == 0 else 1 for dev_i in range(w_in.ndim)))
+    t1 = lax.all_to_all(jnp.tile(w_in, heap), "row", tiled=True, concat_axis=0, split_axis=0)
+    return t1
 
 
 def extended(block, sides, width):
@@ -56,10 +63,7 @@
     normed = lax.all_gather(
         (centred * local_gain[None, :]).astype(jnp.bfloat16), "col", axis=1, tiled=True
     )
-    value_full, gate_full = (
-        lax.all_gather(w_value, "row", axis=0, tiled=True),
-        lax.all_gather(w_gate, "row", axis=0, tiled=True),
-    )
+    value_full, gate_full = (view_node(w_value), lax.all_gather(w_gate, "row", axis=0, tiled=True))
     value_pre = jnp.dot(normed, value_full, preferred_element_type=jnp.float32)
     gate_pre = jnp.dot(normed, gate_full, preferred_element_type=jnp.float32)
     gate_sig = jax.nn.sigmoid(gate_pre)

time: 865 us -> 835 us (0.965)
  waiting for transfers between devices: 615 us -> 584 us
    all_gather x1 -> x0, waiting for transfers between devices: 24.6 us -> none  [shards(): lax.all_gather(w_value, 'row', axis=0, tiled=True)]
    unnamed x11 -> x10, waiting for transfers between devices: 435 us -> 430 us
  transfers between devices with their start and end apart: 13 -> 13, of which waited for: 8 -> 7; matrix products, arithmetic and copies ran while one was open for 5% -> 5% of each run, Pallas kernels for 0% -> 0%
where the time goes in v1:
time: 835 us
  waiting for transfers between devices  584 us (70%)
  blocking collectives  173 us (21%)
  matrix products  19.6 us (2%)
  other arithmetic  17.5 us (2%)
  local copies, waits for them, and re-layouts  16.6 us (2%)
  between operations  14.8 us (2%)
  starting transfers between devices  9.96 us (1%)
    unnamed x10, waiting for transfers between devices  430 us
    psum x1, blocking collectives, shards(): lax.psum((jnp.sum(wide, axis=1), jnp.sum(wide * wide, axis=1)), 'col')  76.2 us
    psum x1, blocking collectives, shards(): lax.psum((jnp.sum(hat_grad, axis=1), jnp.sum(hat_grad * centred, axis=1))...  72.2 us
    all_gather x1, waiting for transfers between devices, shards(): lax.all_gather((centred * local_gain[None, :]).astype(jnp.bfloat16), 'col...  60.4 us
    all_gather x1, waiting for transfers between devices, shards(): act_full = lax.all_gather(activated, 'col', axis=1, tiled=True)  60.1 us
    reduce_scatter x1, waiting for transfers between devices, shards(): lax.psum_scatter(contract_rows(normed, both_grads).astype(jnp.bfloat16),...  26.7 us
    psum x1, blocking collectives, shards(): grad_kernel, grad_bias = lax.psum((kernel_term, bias_term), 'row')  24.2 us
  transfers between devices with their start and end apart: 13, of which 7 were waited for; matrix products, arithmetic and copies ran while one was open for 5% of the time, Pallas kernels for 0%

profile of v1, /device:TPU:0, one launch (start us, length us, event | category | flops | bytes accessed | tf_op | source)
XLA Modules:
  0.0 834.7 jit_solution(15311750616141069951)
XLA Ops:
  7.2 0.0 all-gather.11.cloned.1.call-start
  7.2 0.7 all-gather.11.cloned.1.call-update
  7.9 0.0 all-gather.7.cloned.1.call-start
  7.9 0.7 all-gather.7.cloned.1.call-update
  8.7 0.0 all-gather.5.cloned.1.call-start
  8.7 0.8 dynamic_slice.3
  9.5 1.1 convert_reduce_fusion.1
  10.5 76.2 %all-reduce.1 = (f32[384]{0:T(512)S(1)}, f32[384]{0:T(512)S(1)}) all-reduce(f32[384]{0:T(512)S(1)} %get-tuple-element.44, f32[384]{0:T(512)S(1)} %get-tuple-element.43), channel_id=1, replica_groups=mesh['row'=8,'col'=32] {'col'}, use_global_device_ids=true, to_apply=%region_3.0 | all-reduce | flops 768 | bytes 6144 | tf_op jit(solution)/shard_map/psum | solution.py:59
  86.8 0.6 copy-done.7
  87.3 1.7 fusion.16
  89.0 0.0 all-gather.5.cloned.1.call-update
  89.1 0.0 reduce-scatter.13.cloned.1.call-start
  89.1 0.0 all-gather.11.cloned.1.call-done
  89.1 2.3 convolution_convert_fusion
  91.4 2.8 copy.16
  94.3 0.9 copy-done.6
  95.1 1.1 tile.2
  96.3 4.3 all-to-all-start
  100.6 0.0 all-gather.9.cloned.1.call-start
  100.7 0.1 fusion.116
  100.7 0.1 slice_reduce_fusion.61
  101.0 0.0 all-gather.7.cloned.1.call-done
  101.0 60.4 %all-gather.5.cloned.1.call-done = bf16[384,4096]{1,0:T(8,128)(2,1)} async-done(((bf16[384,128]{1,0:T(8,128)(2,1)}), bf16[384,4096]{1,0:T(8,128)(2,1)}) %all-gather.5.cloned.1.call-update) | async-done | bytes 3145744 | tf_op jit(solution)/shard_map/all_gather | solution.py:63
  161.4 3.2 fusion.2
  164.6 2.9 multiply_convert_fusion.4
  167.5 1.3 collective-permute-start
  168.8 1.3 collective-permute-start.1
  170.1 0.1 slice_reduce_fusion.60
  170.3 3.3 collective-permute-done.1
  173.6 210.4 %reduce-scatter.13.cloned.1.call-done = bf16[128,384]{1,0:T(8,128)(2,1)} async-done(((bf16[4096,384]{1,0:T(8,128)(2,1)}), bf16[128,384]{1,0:T(8,128)(2,1)}) %reduce-scatter.13.cloned.1.call-update) | async-done | bytes 98320
  384.0 1.0 copy.17
  385.1 3.2 fusion.75
  388.3 0.7 multiply_convert_fusion.3
  389.1 0.0 reduce-scatter.9.cloned.1.call-start
  389.1 0.1 fusion.114
  389.2 0.2 slice_reduce_fusion.30
  389.4 1.3 collective-permute-start.2
  390.7 1.3 collective-permute-start.3
  392.0 0.1 slice_reduce_fusion.29
  392.1 3.3 collective-permute-done.3
  395.5 2.2 multiply_convert_fusion
  397.8 2.7 convolution_convert_fusion.1
  400.4 0.0 reduce-scatter.15.cloned.1.call-start
  400.5 1.0 fusion.124
  401.5 0.2 copy-done.3
  401.7 1.0 add_convert_fusion
  402.7 2.8 copy.18
  405.6 0.2 reduce-scatter.11.cloned.1.call-start
  405.8 60.1 %all-gather.9.cloned.1.call-done = bf16[384,4096]{1,0:T(8,128)(2,1)} async-done(((bf16[384,128]{1,0:T(8,128)(2,1)}), bf16[384,4096]{1,0:T(8,128)(2,1)}) %all-gather.9.cloned.1.call-update) | async-done | bytes 3145744 | tf_op jit(solution)/shard_map/all_gather | solution.py:83
  465.9 3.9 convolution_convert_fusion.2
  469.8 1.7 fusion.73
  471.6 1.9 fusion.77
  473.4 1.8 fusion.79
  475.3 3.0 stack.127
  478.2 26.7 %reduce-scatter.9.cloned.1.call-done = bf16[512,256]{1,0:T(8,128)(2,1)} async-done(((bf16[4096,256]{1,0:T(8,128)(2,1)}), bf16[512,256]{1,0:T(8,128)(2,1)}) %reduce-scatter.9.cloned.1.call-update) | async-done | bytes 262160 | tf_op jit(solution)/shard_map/reduce_scatter | solution.py:128
  504.9 1.8 fusion.121
  506.7 2.9 fusion.3
  509.6 218.0 %reduce-scatter.15.cloned.1.call-done = bf16[128,384]{1,0:T(8,128)(2,1)} async-done(((bf16[4096,384]{1,0:T(8,128)(2,1)}), bf16[128,384]{1,0:T(8,128)(2,1)}) %reduce-scatter.15.cloned.1.call-update) | async-done | bytes 98320
  727.6 1.0 copy.19
  728.6 0.3 fusion.12
  728.9 72.2 %all-reduce = (f32[384]{0:T(512)S(1)}, f32[384]{0:T(512)S(1)}) all-reduce(f32[384]{0:T(512)S(1)} %get-tuple-element.40, f32[384]{0:T(512)S(1)} %get-tuple-element.41), channel_id=1, replica_groups=mesh['row'=8,'col'=32] {'col'}, use_global_device_ids=true, to_apply=%region_9.10 | all-reduce | flops 768 | bytes 6144 | tf_op jit(solution)/shard_map/psum | solution.py:141
  801.1 24.2 %all-reduce.2 = (f32[31,128]{1,0:T(8,128)}, f32[128]{0:T(128)}, f32[128]{0:T(128)}) all-reduce(f32[31,128]{1,0:T(8,128)S(1)} %stack.127, f32[128]{0:T(128)S(1)} %copy-done.36, f32[128]{0:T(128)S(1)} %get-tuple-element.39), channel_id=1, replica_groups=mesh['row'=8,'col'=32] {'row'}, use_global_device_ids=true, to_apply=%region_42.43 | all-reduce | flops 4224 | bytes 33792 | tf_op jit(solution)/shard_map/psum | solution.py:124
  825.3 0.9 fusion.10
  826.2 1.6 convert_element_type.92
  (94 shorter events, 0.4 us)
Async XLA Ops:
  7.2 82.0 %all-gather.11.cloned.1.call-start = ((), (), s32[]{:S(2)}) async-start(), calls=%async_computation.8 | async-start | bytes 1179648 | tf_op jit(solution)/shard_map/all_gather | solution.py:84
  7.9 93.1 %all-gather.7.cloned.1.call-start = ((), (), s32[]{:S(2)}) async-start(), calls=%async_computation.6 | async-start | bytes 1179648 | tf_op jit(solution)/shard_map/all_gather | solution.py:66
  8.7 152.8 %all-gather.5.cloned.1.call-start = ((), (), s32[]{:S(2)}) async-start(), calls=%async_computation.5 | async-start | bytes 3244032 | tf_op jit(solution)/shard_map/all_gather | solution.py:63
  9.5 79.6 %copy-start.34 = (f32[128]{0:T(128)}, f32[128]{0:T(128)S(1)}, u32[]{:S(2)}) copy-start(f32[128]{0:T(128)S(1)} %dynamic_slice.3) | copy-start | bytes 1540
  86.7 0.6 copy-start.7
  86.7 0.6 copy-start.9
  89.1 294.9 %reduce-scatter.13.cloned.1.call-start = ((), (), s32[]{:S(2)}) async-start(), calls=%async_computation.11 | async-start | bytes 3244032
  94.2 0.9 copy-start.6
  94.2 6.6 copy-start.33
  96.3 68.3 %all-to-all-start = ((bf16[8,512,128]{2,1,0:T(8,128)(2,1)}), bf16[8,512,128]{2,1,0:T(8,128)(2,1)S(1)}, u32[]{:S(2)}, u32[]{:S(2)}) async-start(bf16[8,512,128]{2,1,0:T(8,128)(2,1)} %tile.2), calls=%async_computation | async-start | bytes 2097152 | tf_op jit(solution)/shard_map/all_to_all | solution.py:14
  100.6 365.3 %all-gather.9.cloned.1.call-start = ((), (), s32[]{:S(2)}) async-start(), calls=%async_computation.7 | async-start | bytes 3244032 | tf_op jit(solution)/shard_map/all_gather | solution.py:83
  100.8 284.1 %copy-start.11 = (f32[384]{0:T(512)}, f32[384]{0:T(512)S(1)}, u32[]{:S(2)}) copy-start(f32[384]{0:T(512)S(1)} %get-tuple-element.77) | copy-start | bytes 4612
  100.9 284.1 %copy-start.12 = (f32[384]{0:T(512)}, f32[384]{0:T(512)S(1)}, u32[]{:S(2)}) copy-start(f32[384]{0:T(512)S(1)} %get-tuple-element.78) | copy-start | bytes 4612
  100.9 284.1 %copy-start.13 = (f32[384]{0:T(512)}, f32[384]{0:T(512)S(1)}, u32[]{:S(2)}) copy-start(f32[384]{0:T(512)S(1)} %get-tuple-element.91) | copy-start | bytes 4612
  100.9 284.1 %copy-start.14 = (f32[384]{0:T(512)}, f32[384]{0:T(512)S(1)}, u32[]{:S(2)}) copy-start(f32[384]{0:T(512)S(1)} %get-tuple-element.92) | copy-start | bytes 4612
  100.9 284.1 %copy-start.15 = (f32[384]{0:T(512)}, f32[384]{0:T(512)S(1)}, u32[]{:S(2)}) copy-start(f32[384]{0:T(512)S(1)} %get-tuple-element.93) | copy-start | bytes 4612
  100.9 284.1 %copy-start.16 = (f32[384]{0:T(512)}, f32[384]{0:T(512)S(1)}, u32[]{:S(2)}) copy-start(f32[384]{0:T(512)S(1)} %get-tuple-element.94) | copy-start | bytes 4612
  100.9 284.1 %copy-start.17 = (f32[384]{0:T(512)}, f32[384]{0:T(512)S(1)}, u32[]{:S(2)}) copy-start(f32[384]{0:T(512)S(1)} %get-tuple-element.76) | copy-start | bytes 4612
  100.9 284.1 %copy-start.18 = (f32[384]{0:T(512)}, f32[384]{0:T(512)S(1)}, u32[]{:S(2)}) copy-start(f32[384]{0:T(512)S(1)} %get-tuple-element.80) | copy-start | bytes 4612
  100.9 284.1 %copy-start.19 = (f32[384]{0:T(512)}, f32[384]{0:T(512)S(1)}, u32[]{:S(2)}) copy-start(f32[384]{0:T(512)S(1)} %get-tuple-element.81) | copy-start | bytes 4612
  100.9 284.1 %copy-start.20 = (f32[384]{0:T(512)}, f32[384]{0:T(512)S(1)}, u32[]{:S(2)}) copy-start(f32[384]{0:T(512)S(1)} %get-tuple-element.82) | copy-start | bytes 4612
  164.6 220.5 %copy-start.37 = (f32[128]{0:T(128)S(1)}, f32[128]{0:T(128)}, u32[]{:S(2)}) copy-start(f32[128]{0:T(128)} %param.13) | copy-start | bytes 1540
  167.5 2.8 collective-permute-start
  168.8 4.8 collective-permute-start.1
  170.2 218.1 %copy-start.21 = (f32[384]{0:T(512)}, f32[384]{0:T(512)S(1)}, u32[]{:S(2)}) copy-start(f32[384]{0:T(512)S(1)} %get-tuple-element.95) | copy-start | bytes 4612
  170.2 218.1 %copy-start.22 = (f32[384]{0:T(512)}, f32[384]{0:T(512)S(1)}, u32[]{:S(2)}) copy-start(f32[384]{0:T(512)S(1)} %get-tuple-element.100) | copy-start | bytes 4612
  170.2 218.1 %copy-start.23 = (f32[384]{0:T(512)}, f32[384]{0:T(512)S(1)}, u32[]{:S(2)}) copy-start(f32[384]{0:T(512)S(1)} %get-tuple-element.101) | copy-start | bytes 4612
  170.2 218.1 %copy-start.24 = (f32[384]{0:T(512)}, f32[384]{0:T(512)S(1)}, u32[]{:S(2)}) copy-start(f32[384]{0:T(512)S(1)} %get-tuple-element.102) | copy-start | bytes 4612
  170.2 218.1 %copy-start.25 = (f32[384]{0:T(512)}, f32[384]{0:T(512)S(1)}, u32[]{:S(2)}) copy-start(f32[384]{0:T(512)S(1)} %get-tuple-element.103) | copy-start | bytes 4612
  170.2 218.1 %copy-start.26 = (f32[384]{0:T(512)}, f32[384]{0:T(512)S(1)}, u32[]{:S(2)}) copy-start(f32[384]{0:T(512)S(1)} %get-tuple-element.104) | copy-start | bytes 4612
  170.2 218.1 %copy-start.27 = (f32[384]{0:T(512)}, f32[384]{0:T(512)S(1)}, u32[]{:S(2)}) copy-start(f32[384]{0:T(512)S(1)} %get-tuple-element.105) | copy-start | bytes 4612
  170.2 218.1 %copy-start.28 = (f32[384]{0:T(512)}, f32[384]{0:T(512)S(1)}, u32[]{:S(2)}) copy-start(f32[384]{0:T(512)S(1)} %get-tuple-element.106) | copy-start | bytes 4612
  170.2 218.1 %copy-start.29 = (f32[384]{0:T(512)}, f32[384]{0:T(512)S(1)}, u32[]{:S(2)}) copy-start(f32[384]{0:T(512)S(1)} %get-tuple-element.96) | copy-start | bytes 4612
  170.3 218.1 %copy-start.30 = (f32[384]{0:T(512)}, f32[384]{0:T(512)S(1)}, u32[]{:S(2)}) copy-start(f32[384]{0:T(512)S(1)} %get-tuple-element.97) | copy-start | bytes 4612
  170.3 218.1 %copy-start.31 = (f32[384]{0:T(512)}, f32[384]{0:T(512)S(1)}, u32[]{:S(2)}) copy-start(f32[384]{0:T(512)S(1)} %get-tuple-element.98) | copy-start | bytes 4612
  170.3 218.1 %copy-start.32 = (f32[384]{0:T(512)}, f32[384]{0:T(512)S(1)}, u32[]{:S(2)}) copy-start(f32[384]{0:T(512)S(1)} %get-tuple-element.99) | copy-start | bytes 4612
  389.1 115.8 %reduce-scatter.9.cloned.1.call-start = ((), (), s32[]{:S(2)}) async-start(), calls=%async_computation.9 | async-start | bytes 2359296 | tf_op jit(solution)/shard_map/reduce_scatter | solution.py:128
  389.4 2.7 collective-permute-start.2
  390.7 4.7 collective-permute-start.3
  395.5 2.3 copy-start.1
  400.4 327.2 %reduce-scatter.15.cloned.1.call-start = ((), (), s32[]{:S(2)}) async-start(), calls=%async_computation.12 | async-start | bytes 3244032
  400.5 1.2 copy-start.3
  405.5 60.4 %copy-start.4 = (bf16[384,128]{1,0:T(8,128)(2,1)S(1)}, bf16[384,128]{1,0:T(8,128)(2,1)}, u32[]{:S(2)}) copy-start(bf16[384,128]{1,0:T(8,128)(2,1)} %param.15) | copy-start | bytes 294916
  405.6 420.6 %reduce-scatter.11.cloned.1.call-start = ((), (), s32[]{:S(2)}) async-start(), calls=%async_computation.10 | async-start | bytes 1179648 | tf_op jit(solution)/shard_map/reduce_scatter | solution.py:92
  469.8 36.9 %copy-start = (bf16[384,4096]{1,0:T(8,128)(2,1)S(1)}, bf16[384,4096]{1,0:T(8,128)(2,1)}, u32[]{:S(2)}) copy-start(bf16[384,4096]{1,0:T(8,128)(2,1)} %all-gather.9.cloned.1.call-done) | copy-start | bytes 9437188
  469.8 36.9 %copy-start.2 = (bf16[384,128]{1,0:T(8,128)(2,1)S(1)}, bf16[384,128]{1,0:T(8,128)(2,1)}, u32[]{:S(2)}) copy-start(bf16[384,128]{1,0:T(8,128)(2,1)} %param.8) | copy-start | bytes 294916
  475.3 253.3 %copy-start.8 = (f32[384]{0:T(512)S(1)}, f32[384]{0:T(512)}, u32[]{:S(2)}) copy-start(f32[384]{0:T(512)} %copy-done.7) | copy-start | bytes 4612
  475.3 253.4 %copy-start.10 = (f32[384]{0:T(512)S(1)}, f32[384]{0:T(512)}, u32[]{:S(2)}) copy-start(f32[384]{0:T(512)} %copy-done.9) | copy-start | bytes 4612
  475.3 253.4 %copy-start.35 = (f32[128]{0:T(128)S(1)}, f32[128]{0:T(128)}, u32[]{:S(2)}) copy-start(f32[128]{0:T(128)} %copy-done.34) | copy-start | bytes 1540
  475.3 325.8 %copy-start.36 = (f32[128]{0:T(128)S(1)}, f32[128]{0:T(128)}, u32[]{:S(2)}) copy-start(f32[128]{0:T(128)} %get-tuple-element.42) | copy-start | bytes 1540
  475.3 350.0 %copy-start.5 = (bf16[384,128]{1,0:T(8,128)(2,1)S(1)}, bf16[384,128]{1,0:T(8,128)(2,1)}, u32[]{:S(2)}) copy-start(bf16[384,128]{1,0:T(8,128)(2,1)} %param.15) | copy-start | bytes 294916
Sparse Core Ops, SparseCore 0:
  9.9 27.1 all-gather.10
  38.9 25.7 all-gather.6
  89.2 72.1 all-gather.4
  165.1 218.7 reduce-scatter.12
  389.2 76.6 all-gather.8
  468.5 36.3 reduce-scatter.8
  509.3 218.2 reduce-scatter.14
  730.1 32.9 reduce-scatter.10
